TPU v7x, 512 devices: a whole 4x4x16 slice. The times are simulated.
512 devices in a mesh: tok: 64 (over y_lo, z, core), head: 8 (over y_hi, x).
Axes of the slice: x: 4, y: 4 (y_hi: 2, y_lo: 2; y = y_hi * 2 + y_lo), z: 16, core: 2. Of those that a mesh axis runs over, the one named last changes fastest.
Arguments:
- tokens: bfloat16 [8192, 3072], P('tok', 'head'), may hold values from -6 to 6
- norm_gain: bfloat16 [3072], replicated, may hold values from 0.099609375 to 1.8984375
- w_query: bfloat16 [3072, 3072], P('tok', 'head'), may hold values from -0.3125 to 0.3125
- w_key: bfloat16 [3072, 1024], P('tok', 'head'), may hold values from -0.3125 to 0.3125
- w_value: bfloat16 [3072, 1024], P('tok', 'head'), may hold values from -0.3125 to 0.3125
- w_out: bfloat16 [3072, 3072], P('tok', 'head'), may hold values from -0.109375 to 0.109375
- cache_keys: bfloat16 [64, 512, 1024], P(None, 'tok', 'head')
- cache_values: bfloat16 [64, 512, 1024], P(None, 'tok', 'head'), may hold values from -18 to 18
- lengths: int32 [64], P('tok'), may hold values from 2 to 512, as said below
- page_table: int32 [64, 32], P('tok'), may hold values from 0 to 31, each once within a row
Outputs:
- mixed: bfloat16 [8192, 3072], P('tok', 'head')
- decode_keys: bfloat16 [2048, 16, 1024], P('tok', None, 'head')
- decode_values: bfloat16 [2048, 16, 1024], P('tok', None, 'head')
Inputs may be any that keep to these rules, and one draw needn't show every extreme that they name: lengths are 2 or more, and some request has exactly 512. Each row of page_table names every page slot once.
All inputs are finite; a program needn't handle non-finite values.
Results may differ from a plain program's by a relative error of at most 0.018.
Values may be sent and summed in bfloat16 or wider, within the bound.
A program may use at most 64 MiB of HBM per device.

v0:
```python
import math
import jax
import jax.numpy as jnp
from jax import lax
from jax.sharding import PartitionSpec as P

HD = 128
rope_base = 500000.0
norm_eps = 1e-05


def rotate(values, positions, head_size):
    row_count = values.shape[0]
    shaped = values.reshape(row_count, -1, head_size)
    half_size = head_size // 2
    exponent = jnp.arange(half_size, dtype=jnp.float32) * (2.0 / head_size)
    frequency = jnp.exp(-math.log(rope_base) * exponent)
    angles = positions.astype(jnp.float32)[:, None] * frequency[None, :]
    cosine = jnp.cos(angles)[:, None, :]
    sine_part = jnp.sin(angles)[:, None, :]
    first_half = shaped[:, :, :half_size]
    second_half = shaped[:, :, half_size:]
    turned = jnp.concatenate(
        [
            first_half * cosine - second_half * sine_part,
            second_half * cosine + first_half * sine_part,
        ],
        axis=2,
    )
    return turned.reshape(row_count, -1)


def attend_head(queries, cached_keys, cached_values, span_keys, span_values, live_slots, causal):
    score_scale = 1.0 / math.sqrt(queries.shape[1])
    numbers = (((1,), (1,)), ((), ()))
    cached_scores = (
        lax.dot_general(queries, cached_keys, numbers, preferred_element_type=jnp.float32)
        * score_scale
    )
    span_scores = (
        lax.dot_general(queries, span_keys, numbers, preferred_element_type=jnp.float32)
        * score_scale
    )
    cached_scores = jnp.where(live_slots[None, :], cached_scores, -jnp.inf)
    span_scores = jnp.where(causal, span_scores, -jnp.inf)
    row_max = jnp.maximum(jnp.max(cached_scores, axis=1), jnp.max(span_scores, axis=1))[:, None]
    cached_exp = jnp.exp(cached_scores - row_max)
    span_exp = jnp.exp(span_scores - row_max)
    row_total = jnp.sum(cached_exp, axis=1, keepdims=True) + jnp.sum(
        span_exp, axis=1, keepdims=True
    )
    cached_weights = (cached_exp / row_total).astype(jnp.bfloat16)
    span_weights = (span_exp / row_total).astype(jnp.bfloat16)
    head_out = jnp.dot(cached_weights, cached_values, preferred_element_type=jnp.float32)
    head_out = head_out + jnp.dot(span_weights, span_values, preferred_element_type=jnp.float32)
    return head_out.astype(jnp.bfloat16)


def shards(
    tokens, norm_gain, w_query, w_key, w_value, w_out, cache_keys, cache_values, lengths, page_table
):
    full_rows = lax.all_gather(tokens, "head", axis=1, tiled=True)
    span_len = full_rows.shape[0]
    as_float = full_rows.astype(jnp.float32)
    mean_square = jnp.mean(as_float * as_float, axis=1, keepdims=True)
    normed = (
        as_float * lax.rsqrt(mean_square + norm_eps) * norm_gain.astype(jnp.float32)[None, :]
    ).astype(jnp.bfloat16)

    def add_rows(weight_rows):
        return jnp.dot(normed, weight_rows, preferred_element_type=jnp.float32)

    query_sum = add_rows(lax.all_gather(w_query, "tok", axis=0, tiled=True))
    key_sum = add_rows(lax.all_gather(w_key, "tok", axis=0, tiled=True))
    value_sum = add_rows(lax.all_gather(w_value, "tok", axis=0, tiled=True))
    length = lengths[0]
    positions = length + jnp.arange(span_len, dtype=jnp.int32)
    queries = rotate(query_sum, positions, HD).astype(jnp.bfloat16)
    key_new = rotate(key_sum, positions, HD).astype(jnp.bfloat16)
    value_new = value_sum.astype(jnp.bfloat16)
    moved_keys, moved_values = (
        lax.all_to_all(cache_keys, "tok", split_axis=0, concat_axis=1, tiled=True),
        lax.all_to_all(cache_values, "tok", split_axis=0, concat_axis=1, tiled=True),
    )
    slot_total = moved_keys.shape[1]
    live_slots = jnp.arange(slot_total, dtype=jnp.int32) < length
    keys_live = jnp.where(live_slots[:, None], moved_keys[0], jnp.zeros_like(moved_keys[0]))
    values_live = jnp.where(live_slots[:, None], moved_values[0], jnp.zeros_like(moved_values[0]))
    slot_count = page_table.shape[1]
    page_keys = keys_live.reshape(slot_count, -1, keys_live.shape[1])
    page_values = values_live.reshape(slot_count, -1, values_live.shape[1])
    decode_keys = jnp.zeros_like(page_keys).at[page_table[0]].set(page_keys)
    decode_values = jnp.zeros_like(page_values).at[page_table[0]].set(page_values)
    token_ids = jnp.arange(span_len, dtype=jnp.int32)
    causal = token_ids[None, :] <= token_ids[:, None]
    local_heads = queries.shape[1] // HD

    def one_head(head_number):
        head_start = head_number * HD
        return attend_head(
            lax.dynamic_slice_in_dim(queries, head_start, HD, 1),
            keys_live,
            values_live,
            key_new,
            value_new,
            live_slots,
            causal,
        )

    heads_out = lax.map(one_head, jnp.arange(local_heads, dtype=jnp.int32))
    attention = jnp.transpose(heads_out, (1, 0, 2)).reshape(span_len, local_heads * HD)
    partial_out = lax.dot_general(
        attention,
        lax.all_gather(w_out, "tok", axis=0, tiled=True),
        (((1,), (1,)), ((), ())),
        preferred_element_type=jnp.float32,
    )
    mixed = lax.psum_scatter(
        partial_out.astype(jnp.bfloat16), "head", scatter_dimension=1, tiled=True
    )
    return (mixed, decode_keys, decode_values)


def solution(mesh):
    in_specs = (
        P("tok", "head"),
        P(),
        P("tok", "head"),
        P("tok", "head"),
        P("tok", "head"),
        P("tok", "head"),
        P(None, "tok", "head"),
        P(None, "tok", "head"),
        P("tok"),
        P("tok", None),
    )
    out_specs = (P("tok", "head"), P("tok", None, "head"), P("tok", None, "head"))
    return jax.shard_map(shards, mesh=mesh, in_specs=in_specs, out_specs=out_specs, check_vma=False)
```

profile of v0, /device:TPU:2, one launch (start us, length us, event | category | flops | bytes accessed | tf_op | source)
XLA Modules:
  0.0 356.6 jit_solution(9091315769664037303)
XLA Ops:
  7.2 0.7 all-gather.3.cloned.1.call-update
  7.9 17.1 %all-to-all-start = ((bf16[64,8,128]{2,1,0:T(8,128)(2,1)}), bf16[64,8,128]{2,1,0:T(8,128)(2,1)S(1)}, u32[]{:S(2)}, u32[]{:S(2)}) async-start(bf16[64,8,128]{2,1,0:T(8,128)(2,1)} %param.18), calls=%async_computation | async-start | bytes 262144 | tf_op jit(solution)/shard_map/all_to_all | solution.py:82
  25.1 0.7 all-gather.5.cloned.1.call-update
  25.8 36.2 %all_gather.15 = bf16[128,3072]{1,0:T(8,128)(2,1)S(1)} all-gather(bf16[128,384]{1,0:T(8,128)(2,1)} %param.12), channel_id=1, replica_groups=mesh['tok'=64,'head'=8] {'head'}, dimensions={1}, use_global_device_ids=true | all-gather | bytes 884736 | tf_op jit(solution)/shard_map/all_gather | solution.py:62
  62.0 0.2 fusion.17
  62.9 64.6 %all_gather.17 = bf16[3072,128]{1,0:T(8,128)(2,1)S(1)} all-gather(bf16[48,128]{1,0:T(8,128)(2,1)S(1)} %copy-done.2), channel_id=1, replica_groups=mesh['tok'=64,'head'=8] {'tok'}, dimensions={0}, use_global_device_ids=true | all-gather | bytes 798720 | tf_op jit(solution)/shard_map/all_gather | solution.py:74
  127.5 0.5 convolution_bitcast_fusion
  128.0 0.2 fusion.25
  128.3 61.8 %all_gather.18 = bf16[3072,128]{1,0:T(8,128)(2,1)S(1)} all-gather(bf16[48,128]{1,0:T(8,128)(2,1)S(1)} %copy-done.3), channel_id=1, replica_groups=mesh['tok'=64,'head'=8] {'tok'}, dimensions={0}, use_global_device_ids=true | all-gather | bytes 798720 | tf_op jit(solution)/shard_map/all_gather | solution.py:75
  190.1 4.6 %all-to-all-start.1 = ((bf16[64,8,128]{2,1,0:T(8,128)(2,1)}), bf16[64,8,128]{2,1,0:T(8,128)(2,1)S(1)}, u32[]{:S(2)}, u32[]{:S(2)}) async-start(bf16[64,8,128]{2,1,0:T(8,128)(2,1)} %param.19), calls=%async_computation.1 | async-start | bytes 262144 | tf_op jit(solution)/shard_map/all_to_all | solution.py:83
  194.8 0.1 copy.20
  194.9 0.2 multiply_cosine_fusion.1
  195.1 0.4 convolution_convert_fusion.1
  195.5 17.0 %all-to-all-done.1 = bf16[64,8,128]{2,1,0:T(8,128)(2,1)S(1)} async-done(((bf16[64,8,128]{2,1,0:T(8,128)(2,1)}), bf16[64,8,128]{2,1,0:T(8,128)(2,1)S(1)}, u32[]{:S(2)}, u32[]{:S(2)}) %all-to-all-start.1) | async-done | bytes 131104 | tf_op jit(solution)/shard_map/all_to_all | solution.py:83
  212.5 0.1 bitcast_select_fusion.2
  212.7 2.7 fusion.31
  215.5 9.7 %while.11 = (s32[]{:T(128)}, bf16[3,128,128]{1,2,0:T(8,128)(2,1)S(1)}, s32[3]{0:T(128)S(1)}, bf16[128,384]{0,1:T(8,128)(2,1)S(1)}, bf16[512,128]{1,0:T(8,128)(2,...) while((s32[]{:T(128)}, ...), condition=%wide.region_6.7_spmd.clone, body=%wide.region_1.6_spmd.clone.sunk | while | flops 42647812 | bytes 1680583 | solution.py:110
  215.5 0.6 dynamic_slice.22
  216.8 0.7 iota_compare_fusion.4
  217.4 0.3 fusion.58
  217.7 0.2 fusion.59
  217.9 0.2 fusion.60
  218.1 0.3 fusion.62
  218.4 0.2 fusion.63
  218.6 0.1 copy.29
  218.8 0.6 dynamic_slice.22
  220.0 0.7 iota_compare_fusion.4
  220.7 0.3 fusion.58
  221.0 0.2 fusion.59
  221.2 0.2 fusion.60
  221.4 0.3 fusion.62
  221.6 0.2 fusion.63
  221.8 0.1 copy.29
  222.0 0.6 dynamic_slice.22
  223.2 0.7 iota_compare_fusion.4
  223.9 0.3 fusion.58
  224.2 0.2 fusion.59
  224.4 0.2 fusion.60
  224.6 0.3 fusion.62
  224.9 0.2 fusion.63
  225.2 35.4 %all-gather.5.cloned.1.call-done = bf16[3072,384]{1,0:T(8,128)(2,1)} async-done(((bf16[48,384]{1,0:T(8,128)(2,1)}), bf16[3072,384]{1,0:T(8,128)(2,1)}) %all-gather.5.cloned.1.call-update) | async-done | bytes 2359312 | tf_op jit(solution)/shard_map/all_gather | solution.py:114
  260.7 2.6 convolution_convert_fusion
  263.3 1.2 copy.23
  264.5 0.1 bitcast_select_fusion
  264.7 1.5 scatter_fusion
  266.2 1.5 scatter_fusion.1
  267.7 80.7 %reduce-scatter.4.cloned.1.call-done = bf16[384,128]{1,0:T(8,128)(2,1)} async-done(((bf16[3072,128]{1,0:T(8,128)(2,1)}), bf16[384,128]{1,0:T(8,128)(2,1)}) %reduce-scatter.4.cloned.1.call-update) | async-done | bytes 98320
  348.5 1.6 copy.24
  (45 shorter events, 0.7 us)
Async XLA Ops:
  7.2 55.1 %copy-start.4 = (bf16[3072]{0:T(1024)(128)(2,1)S(1)}, bf16[3072]{0:T(1024)(128)(2,1)}, u32[]{:S(2)}) copy-start(bf16[3072]{0:T(1024)(128)(2,1)} %param.13) | copy-start | bytes 18436
  7.2 55.8 %copy-start.2 = (bf16[48,128]{1,0:T(8,128)(2,1)S(1)}, bf16[48,128]{1,0:T(8,128)(2,1)}, u32[]{:S(2)}) copy-start(bf16[48,128]{1,0:T(8,128)(2,1)} %param.15) | copy-start | bytes 36868
  7.2 205.5 %all-gather.3.cloned.1.call-start = ((), (), s32[]{:S(2)}) async-start(), calls=%async_computation.3 | async-start | bytes 2396160 | tf_op jit(solution)/shard_map/all_gather | solution.py:73
  7.9 182.1 %all-to-all-start = ((bf16[64,8,128]{2,1,0:T(8,128)(2,1)}), bf16[64,8,128]{2,1,0:T(8,128)(2,1)S(1)}, u32[]{:S(2)}, u32[]{:S(2)}) async-start(bf16[64,8,128]{2,1,0:T(8,128)(2,1)} %param.18), calls=%async_computation | async-start | bytes 262144 | tf_op jit(solution)/shard_map/all_to_all | solution.py:82
  25.1 235.6 %all-gather.5.cloned.1.call-start = ((), (), s32[]{:S(2)}) async-start(), calls=%async_computation.4 | async-start | bytes 2396160 | tf_op jit(solution)/shard_map/all_gather | solution.py:114
  62.2 66.0 %copy-start.3 = (bf16[48,128]{1,0:T(8,128)(2,1)S(1)}, bf16[48,128]{1,0:T(8,128)(2,1)}, u32[]{:S(2)}) copy-start(bf16[48,128]{1,0:T(8,128)(2,1)} %param.16) | copy-start | bytes 36868
  190.1 22.5 %all-to-all-start.1 = ((bf16[64,8,128]{2,1,0:T(8,128)(2,1)}), bf16[64,8,128]{2,1,0:T(8,128)(2,1)S(1)}, u32[]{:S(2)}, u32[]{:S(2)}) async-start(bf16[64,8,128]{2,1,0:T(8,128)(2,1)} %param.19), calls=%async_computation.1 | async-start | bytes 262144 | tf_op jit(solution)/shard_map/all_to_all | solution.py:83
  194.7 153.8 %reduce-scatter.4.cloned.1.call-start = ((), (), s32[]{:S(2)}) async-start(), calls=%async_computation.5 | async-start | bytes 884736
  263.2 1.2 copy-start.5
  266.2 83.9 %copy-start.1 = (bf16[32,16,128]{2,1,0:T(8,128)(2,1)}, bf16[32,16,128]{2,1,0:T(8,128)(2,1)S(1)}, u32[]{:S(2)}) copy-start(bf16[32,16,128]{2,1,0:T(8,128)(2,1)S(1)} %scatter_fusion) | copy-start | bytes 393220
  267.7 82.4 %copy-start = (bf16[32,16,128]{2,1,0:T(8,128)(2,1)}, bf16[32,16,128]{2,1,0:T(8,128)(2,1)S(1)}, u32[]{:S(2)}) copy-start(bf16[32,16,128]{2,1,0:T(8,128)(2,1)S(1)} %scatter_fusion.1) | copy-start | bytes 393220
Sparse Core Ops, SparseCore 0:
  10.2 127.4 all-gather.2
  139.8 120.8 all-gather.4
  265.2 83.2 reduce-scatter.3
where the time goes:
time: 357 us
  blocking collectives  163 us (46%)
  waiting for transfers between devices  135 us (38%)
  starting transfers between devices  21.9 us (6%)
  between operations  14.7 us (4%)
  matrix products  9 us (3%)
  local copies, waits for them, and re-layouts  8.13 us (2%)
  other arithmetic  3.71 us (1%)
    unnamed x4, waiting for transfers between devices  82.1 us
    all_gather x1, blocking collectives, shards(): key_sum = add_rows(lax.all_gather(w_key, 'tok', axis=0, tiled=True))  64.6 us
    all_gather x1, blocking collectives, shards(): value_sum = add_rows(lax.all_gather(w_value, 'tok', axis=0, tiled=True))  61.8 us
    all_gather x1, blocking collectives, shards(): full_rows = lax.all_gather(tokens, 'head', axis=1, tiled=True)  36.2 us
    all_gather x1, waiting for transfers between devices, shards(): lax.all_gather(w_out, 'tok', axis=0, tiled=True)  35.4 us
    all_to_all x1, starting transfers between devices, shards(): lax.all_to_all(cache_keys, 'tok', split_axis=0, concat_axis=1, tiled=True)  17.1 us
    all_to_all x1, waiting for transfers between devices, shards(): lax.all_to_all(cache_values, 'tok', split_axis=0, concat_axis=1, tiled=True)  17 us
  transfers between devices with their start and end apart: 5, of which 3 were waited for; matrix products, arithmetic and copies ran while one was open for 4% of the time, Pallas kernels for 0%

commit v1 on v0

--- a/solution.py
+++ b/solution.py
@@ -111,7 +111,9 @@
     attention = jnp.transpose(heads_out, (1, 0, 2)).reshape(span_len, local_heads * HD)
     partial_out = lax.dot_general(
         attention,
-        lax.all_gather(w_out, "tok", axis=0, tiled=True),
+        jnp.concatenate(
+            jax.lax.all_to_all(jnp.stack(jax.lax.axis_size("tok") * [w_out]), "tok", 0, 0), axis=0
+        ),
         (((1,), (1,)), ((), ())),
         preferred_element_type=jnp.float32,
     )

time: 357 us -> 416 us (1.17)
  blocking collectives: 163 us -> 285 us
  waiting for transfers between devices: 135 us -> 76.9 us
  starting transfers between devices: 21.9 us -> 4.91 us
  local copies, waits for them, and re-layouts: 8.13 us -> 13 us
  matrix products: 9 us -> 13.8 us
    all_gather x1, blocking collectives: 64.6 us -> 131 us  [shards(): key_sum = add_rows(lax.all_gather(w_key, 'tok', axis=0, tiled=True))]
    all_to_all x0 -> x2, blocking collectives: none -> 55.9 us  [the longest x1 34.2 us: shards(): lax.all_to_all(cache_keys, 'tok', split_axis=0, concat_axis=1, tiled=True)]
    all_gather x1 -> x0, waiting for transfers between devices: 35.4 us -> none  [shards(): lax.all_gather(w_out, 'tok', axis=0, tiled=True)]
    all_to_all x2 -> x1, waiting for transfers between devices: 17 us -> 0.01 us  [shards(): jax.lax.all_to_all(jnp.stack(jax.lax.axis_size('tok') * [w_out]), 'tok',...]
    all_to_all x2 -> x1, starting transfers between devices: 21.7 us -> 4.83 us  [shards(): jax.lax.all_to_all(jnp.stack(jax.lax.axis_size('tok') * [w_out]), 'tok',...]
    unnamed x4 -> x3, waiting for transfers between devices: 82.1 us -> 76.9 us
  transfers between devices with their start and end apart: 5 -> 3, of which waited for: 3 -> 1; matrix products, arithmetic and copies ran while one was open for 4% -> 6% of each run, Pallas kernels for 0% -> 0%
where the time goes in v1:
time: 416 us; the launch traced here: 415 us
  blocking collectives  285 us (69%)
  waiting for transfers between devices  76.9 us (18%)
  between operations  14.9 us (4%)
  matrix products  13.8 us (3%)
  local copies, waits for them, and re-layouts  13 us (3%)
  other arithmetic  4.98 us (1%)
  starting transfers between devices  4.91 us (1%)
    all_gather x1, blocking collectives, shards(): key_sum = add_rows(lax.all_gather(w_key, 'tok', axis=0, tiled=True))  131 us
    unnamed x3, waiting for transfers between devices  76.9 us
    all_gather x1, blocking collectives, shards(): value_sum = add_rows(lax.all_gather(w_value, 'tok', axis=0, tiled=True))  61.7 us
    all_gather x1, blocking collectives, shards(): full_rows = lax.all_gather(tokens, 'head', axis=1, tiled=True)  36.4 us
    all_to_all x1, blocking collectives, shards(): lax.all_to_all(cache_keys, 'tok', split_axis=0, concat_axis=1, tiled=True)  34.2 us
    all_to_all x1, blocking collectives, shards(): lax.all_to_all(cache_values, 'tok', split_axis=0, concat_axis=1, tiled=True)  21.7 us
  transfers between devices with their start and end apart: 3, of which 1 were waited for; matrix products, arithmetic and copies ran while one was open for 6% of the time, Pallas kernels for 0%

profile of v1, /device:TPU:2, one launch (start us, length us, event | category | flops | bytes accessed | tf_op | source)
XLA Modules:
  0.0 415.2 jit_solution(937361261031181933)
XLA Ops:
  7.2 34.2 %all_to_all.23 = bf16[64,8,128]{2,1,0:T(8,128)(2,1)S(1)} all-to-all(bf16[64,8,128]{2,1,0:T(8,128)(2,1)} %param.18), channel_id=1, replica_groups=mesh['tok'=64,'head'=8] {'tok'}, dimensions={0} | all-to-all | bytes 262144 | tf_op jit(solution)/shard_map/all_to_all | solution.py:82
  41.4 21.7 %all_to_all.24 = bf16[64,8,128]{2,1,0:T(8,128)(2,1)S(1)} all-to-all(bf16[64,8,128]{2,1,0:T(8,128)(2,1)} %param.19), channel_id=1, replica_groups=mesh['tok'=64,'head'=8] {'tok'}, dimensions={0} | all-to-all | bytes 262144 | tf_op jit(solution)/shard_map/all_to_all | solution.py:83
  63.1 2.4 stack.2
  65.5 4.8 %all-to-all-start.2 = ((bf16[64,48,384]{2,1,0:T(8,128)(2,1)}), bf16[64,48,384]{2,1,0:T(8,128)(2,1)S(1)}, u32[]{:S(2)}, u32[]{:S(2)}) async-start(bf16[64,48,384]{2,1,0:T(8,128)(2,1)} %stack.2), calls=%async_computation.2 | async-start | bytes 4718592 | tf_op jit(solution)/shard_map/all_to_all | solution.py:115
  70.4 0.7 all-gather.2.cloned.1.call-update
  71.8 36.4 %all_gather.12 = bf16[128,3072]{1,0:T(8,128)(2,1)S(1)} all-gather(bf16[128,384]{1,0:T(8,128)(2,1)S(1)} %copy-done.4), channel_id=1, replica_groups=mesh['tok'=64,'head'=8] {'head'}, dimensions={1}, use_global_device_ids=true | all-gather | bytes 884736 | tf_op jit(solution)/shard_map/all_gather | solution.py:62
  108.2 0.2 fusion.17
  108.5 130.6 %all_gather.14 = bf16[3072,128]{1,0:T(8,128)(2,1)S(1)} all-gather(bf16[48,128]{1,0:T(8,128)(2,1)S(1)} %copy-done.5), channel_id=1, replica_groups=mesh['tok'=64,'head'=8] {'tok'}, dimensions={0}, use_global_device_ids=true | all-gather | bytes 798720 | tf_op jit(solution)/shard_map/all_gather | solution.py:74
  239.1 0.5 convolution_bitcast_fusion
  239.6 0.2 fusion.25
  239.8 0.7 copy.20
  240.5 0.8 multiply_cosine_fusion.1
  241.3 61.7 %all_gather.15 = bf16[3072,128]{1,0:T(8,128)(2,1)S(1)} all-gather(bf16[48,128]{1,0:T(8,128)(2,1)S(1)} %copy-done.6), channel_id=1, replica_groups=mesh['tok'=64,'head'=8] {'tok'}, dimensions={0}, use_global_device_ids=true | all-gather | bytes 798720 | tf_op jit(solution)/shard_map/all_gather | solution.py:75
  303.0 1.0 convolution_convert_fusion.1
  304.0 0.8 bitcast_select_fusion.2
  304.8 2.7 fusion.31
  307.7 16.5 %while.11 = (s32[]{:T(128)}, bf16[3,128,128]{1,2,0:T(8,128)(2,1)}, s32[3]{0:T(128)S(1)}, bf16[128,384]{0,1:T(8,128)(2,1)S(1)}, bf16[512,128]{1,0:T(8,128)(2,1)S(...) while((s32[]{:T(128)}, bf16[3,128,128]{1,2,0:T(8,128)(2,1)}, ...), condition=%wide.region_6.7_spmd.clone, body=%wide.region_1.6_spmd.clone.sunk | while | flops 42647812 | bytes 1811691 | solution.py:110
  307.7 0.6 dynamic_slice.22
  309.0 0.7 iota_compare_fusion.4
  309.6 0.9 fusion.59
  310.5 0.3 fusion.58
  310.9 0.2 fusion.60
  311.1 1.2 fusion.62
  312.3 0.2 fusion.63
  312.6 0.6 constant_dynamic-update-slice_fusion.2
  313.2 0.6 dynamic_slice.22
  314.5 0.7 iota_compare_fusion.4
  315.1 0.9 fusion.59
  316.0 0.3 fusion.58
  316.4 0.2 fusion.60
  316.6 1.2 fusion.62
  317.8 0.2 fusion.63
  318.1 0.6 constant_dynamic-update-slice_fusion.2
  318.7 0.6 dynamic_slice.22
  320.0 0.7 iota_compare_fusion.4
  320.6 0.9 fusion.59
  321.5 0.3 fusion.58
  321.9 0.2 fusion.60
  322.1 1.2 fusion.62
  323.3 0.2 fusion.63
  323.6 0.6 constant_dynamic-update-slice_fusion.2
  324.2 1.8 convolution_convert_fusion
  326.0 1.2 copy.23
  327.2 0.1 bitcast_select_fusion
  327.4 1.5 scatter_fusion.1
  329.0 1.5 scatter_fusion
  330.5 76.2 %reduce-scatter.4.cloned.1.call-done = bf16[384,128]{1,0:T(8,128)(2,1)} async-done(((bf16[3072,128]{1,0:T(8,128)(2,1)}), bf16[384,128]{1,0:T(8,128)(2,1)}) %reduce-scatter.4.cloned.1.call-update) | async-done | bytes 98320
  406.7 1.6 copy.24
  (55 shorter events, 0.8 us)
Async XLA Ops:
  65.5 6.3 %copy-start.7 = (bf16[3072]{0:T(1024)(128)(2,1)S(1)}, bf16[3072]{0:T(1024)(128)(2,1)}, u32[]{:S(2)}) copy-start(bf16[3072]{0:T(1024)(128)(2,1)} %param.13) | copy-start | bytes 18436
  65.5 6.3 %copy-start.4 = (bf16[128,384]{1,0:T(8,128)(2,1)S(1)}, bf16[128,384]{1,0:T(8,128)(2,1)}, u32[]{:S(2)}) copy-start(bf16[128,384]{1,0:T(8,128)(2,1)} %param.12) | copy-start | bytes 294916
  65.5 258.7 %all-to-all-start.2 = ((bf16[64,48,384]{2,1,0:T(8,128)(2,1)}), bf16[64,48,384]{2,1,0:T(8,128)(2,1)S(1)}, u32[]{:S(2)}, u32[]{:S(2)}) async-start(bf16[64,48,384]{2,1,0:T(8,128)(2,1)} %stack.2), calls=%async_computation.2 | async-start | bytes 4718592 | tf_op jit(solution)/shard_map/all_to_all | solution.py:115
  70.3 38.1 %copy-start.5 = (bf16[48,128]{1,0:T(8,128)(2,1)S(1)}, bf16[48,128]{1,0:T(8,128)(2,1)}, u32[]{:S(2)}) copy-start(bf16[48,128]{1,0:T(8,128)(2,1)} %param.15) | copy-start | bytes 36868
  70.3 234.5 %all-gather.2.cloned.1.call-start = ((), (), s32[]{:S(2)}) async-start(), calls=%async_computation.4 | async-start | bytes 2396160 | tf_op jit(solution)/shard_map/all_gather | solution.py:73
  71.1 335.6 %reduce-scatter.4.cloned.1.call-start = ((), (), s32[]{:S(2)}) async-start(), calls=%async_computation.5 | async-start | bytes 884736
  108.4 132.9 %copy-start.6 = (bf16[48,128]{1,0:T(8,128)(2,1)S(1)}, bf16[48,128]{1,0:T(8,128)(2,1)}, u32[]{:S(2)}) copy-start(bf16[48,128]{1,0:T(8,128)(2,1)} %param.16) | copy-start | bytes 36868
  304.8 2.8 copy-start.2
  304.8 2.8 copy-start.3
  307.7 4.6 %copy-start.9 = (bf16[128,128]{1,0:T(8,128)(2,1)S(1)}, bf16[128,128]{1,0:T(8,128)(2,1)}, u32[]{:S(2)}) copy-start(bf16[128,128]{1,0:T(8,128)(2,1)} %get-tuple-element.233) | copy-start | bytes 98308 | tf_op jit(solution)/shard_map/while
  313.2 4.5 %copy-start.9 = (bf16[128,128]{1,0:T(8,128)(2,1)S(1)}, bf16[128,128]{1,0:T(8,128)(2,1)}, u32[]{:S(2)}) copy-start(bf16[128,128]{1,0:T(8,128)(2,1)} %get-tuple-element.233) | copy-start | bytes 98308 | tf_op jit(solution)/shard_map/while
  318.7 4.5 %copy-start.9 = (bf16[128,128]{1,0:T(8,128)(2,1)S(1)}, bf16[128,128]{1,0:T(8,128)(2,1)}, u32[]{:S(2)}) copy-start(bf16[128,128]{1,0:T(8,128)(2,1)} %get-tuple-element.233) | copy-start | bytes 98308 | tf_op jit(solution)/shard_map/while
  326.0 1.2 copy-start.8
  328.9 79.4 %copy-start.1 = (bf16[32,16,128]{2,1,0:T(8,128)(2,1)}, bf16[32,16,128]{2,1,0:T(8,128)(2,1)S(1)}, u32[]{:S(2)}) copy-start(bf16[32,16,128]{2,1,0:T(8,128)(2,1)S(1)} %scatter_fusion.1) | copy-start | bytes 393220
  330.5 77.9 %copy-start = (bf16[32,16,128]{2,1,0:T(8,128)(2,1)}, bf16[32,16,128]{2,1,0:T(8,128)(2,1)S(1)}, u32[]{:S(2)}) copy-start(bf16[32,16,128]{2,1,0:T(8,128)(2,1)S(1)} %scatter_fusion) | copy-start | bytes 393220
Sparse Core Ops, SparseCore 0:
  73.3 151.9 all-gather.1
  327.3 79.3 reduce-scatter.3
